TPU v7x, 512 devices: a whole 4x4x16 slice. The times are simulated.
512 devices in a mesh: gx: 16 (over y, z_lo), gy: 32 (over x, z_hi, core).
Axes of the slice: x: 4, y: 4, z: 16 (z_hi: 4, z_lo: 4; z = z_hi * 4 + z_lo), core: 2. Of those that a mesh axis runs over, the one named last changes fastest.
Arguments:
- inputs: bfloat16 [128, 128, 8, 128], P('gx', 'gy'), may hold values from -6 to 6
- preact: bfloat16 [128, 128, 8, 128], P('gx', 'gy'), may hold values from -6 to 6
- cotangent: bfloat16 [128, 128, 8, 128], P('gx', 'gy'), may hold values from -6 to 6
- spectral_w: bfloat16 [32, 32, 8, 128, 128], P('gx', 'gy'), may hold values from -2 to 2
- skip_w: bfloat16 [128, 128], replicated, may hold values from -0.5 to 0.5
Outputs:
- grad_inputs: bfloat16 [128, 128, 8, 128], P('gx', 'gy')
- grad_spectral: bfloat16 [32, 32, 8, 128, 128], P('gx', 'gy')
- grad_skip: float32 [128, 128], replicated
All inputs are finite; a program needn't handle non-finite values.
Results may differ from a plain program's by a relative error of at most 0.0054.
Values may be sent and summed in bfloat16 or wider, within the bound.
A program may use at most 64 MiB of HBM per device.

v0:
```python
import math

import jax
import jax.numpy as jnp
from jax import lax
from jax.sharding import PartitionSpec as P

highest = lax.Precision.HIGHEST


def cas_table(modes, length, offset, cells):
    index = jnp.arange(modes, dtype=jnp.int32)
    freq = jnp.where(index < modes // 2, index, length - modes + index)
    where_cells = offset + jnp.arange(cells, dtype=jnp.int32)
    phase = freq[:, None] * where_cells[None, :] % length
    angle = phase.astype(jnp.float32) * (2.0 * math.pi / length)
    return (jnp.cos(angle) + jnp.sin(angle)) / math.sqrt(length)


def on_device(inputs, preact, cotangent, spectral_w, skip_w):
    cells_x, cells_y, cells_z, channels = inputs.shape
    length_x = cells_x * lax.axis_size("gx")
    length_y = cells_y * lax.axis_size("gy")
    local_modes_x, local_modes_y, modes_z = (
        spectral_w.shape[0],
        spectral_w.shape[1],
        spectral_w.shape[2],
    )
    modes_x = local_modes_x * lax.axis_size("gx")
    modes_y = local_modes_y * lax.axis_size("gy")
    table_z = cas_table(modes_z, cells_z, 0, cells_z)
    table_x = cas_table(modes_x, length_x, lax.axis_index("gx") * cells_x, cells_x)
    table_y = cas_table(modes_y, length_y, lax.axis_index("gy") * cells_y, cells_y)
    preact_wide = preact.astype(jnp.float32)
    gelu_slope = 0.5 * (
        1.0 + jax.scipy.special.erf(preact_wide * (1.0 / math.sqrt(2.0)))
    ) + preact_wide * jnp.exp(-0.5 * preact_wide * preact_wide) * (1.0 / math.sqrt(2.0 * math.pi))
    grad_pre = (cotangent.astype(jnp.float32) * gelu_slope).astype(jnp.bfloat16)
    fields = jnp.stack([inputs, grad_pre]).astype(jnp.float32)
    z_modes = jnp.einsum("ck,fijkh->fijch", table_z, fields, precision=highest)
    table_rows = table_x
    part_x = lax.psum_scatter(
        jnp.einsum("ai,fijch->afjch", table_rows, z_modes, precision=highest),
        "gx",
        scatter_dimension=0,
        tiled=True,
    )
    table_rows = table_y
    swapped = lax.psum_scatter(
        jnp.einsum("bj,afjch->bafch", table_rows, part_x, precision=highest),
        "gy",
        scatter_dimension=0,
        tiled=True,
    )
    owned_modes = jnp.swapaxes(swapped, 0, 1)
    input_modes = owned_modes[:, :, 0]
    grad_modes = owned_modes[:, :, 1]
    grad_spectral = jnp.einsum(
        "abcp,abcq->abcpq", input_modes, grad_modes, precision=highest
    ).astype(jnp.bfloat16)
    back_modes = jnp.einsum(
        "abcq,abcpq->abcp", grad_modes, spectral_w.astype(jnp.float32), precision=highest
    ).astype(jnp.bfloat16)
    table_rows = table_y
    over_second = jnp.einsum(
        "bj,abch->ajch",
        table_rows,
        lax.all_gather(back_modes, "gy", axis=1, tiled=True).astype(jnp.float32),
        precision=highest,
    )
    table_rows = table_x
    cell_modes = jnp.einsum(
        "ai,ajch->ijch",
        table_rows,
        lax.all_gather(over_second, "gx", axis=0, tiled=True),
        precision=highest,
    )
    spectral_cells = jnp.einsum("ck,ijch->ijkh", table_z, cell_modes, precision=highest)
    flat_grad = grad_pre.reshape(-1, channels)
    skip_part = lax.dot_general(
        flat_grad, skip_w, (((1,), (1,)), ((), ())), preferred_element_type=jnp.float32
    )
    grad_inputs = (skip_part.reshape(cells_x, cells_y, cells_z, channels) + spectral_cells).astype(
        jnp.bfloat16
    )
    local_sum = lax.dot_general(
        inputs.reshape(-1, channels),
        flat_grad,
        (((0,), (0,)), ((), ())),
        preferred_element_type=jnp.float32,
    )
    grad_skip = lax.psum(local_sum, ("gx", "gy")) / math.sqrt(length_x * length_y * cells_z)
    return (grad_inputs, grad_spectral, grad_skip)


def solution(mesh):
    in_specs = (
        P("gx", "gy", None, None),
        P("gx", "gy", None, None),
        P("gx", "gy", None, None),
        P("gx", "gy", None, None, None),
        P(),
    )
    out_specs = (P("gx", "gy", None, None), P("gx", "gy", None, None, None), P())
    return jax.shard_map(
        on_device, mesh=mesh, in_specs=in_specs, out_specs=out_specs, check_vma=False
    )
```

profile of v0, /device:TPU:1, one launch (start us, length us, event | category | flops | bytes accessed | tf_op | source)
XLA Modules:
  0.0 575.6 jit_solution(9637456103592399393)
XLA Ops:
  8.0 0.0 copy-start
  8.0 0.0 reduce-scatter.3.cloned.1.call-start
  8.1 0.0 copy-start.1
  8.1 1.0 fusion.21
  9.1 0.0 copy-done.1
  9.1 0.4 convolution_bitcast_fusion
  9.5 1.1 fusion.7
  10.6 1.6 copy.23
  12.2 0.0 reduce-scatter.3.cloned.1.call-update
  12.2 0.0 all-reduce.2.cloned.1.call-start
  12.3 0.8 convolution_bitcast_fusion.2
  13.1 0.0 all-reduce.2.cloned.1.call-update
  13.2 0.0 reduce-scatter.5.cloned.1.call-start
  13.2 85.2 %reduce-scatter.3.cloned.1.call-done = f32[2,2,4,8,128]{4,3,2,1,0:T(8,128)} async-done(((f32[32,2,4,8,128]{4,3,2,1,0:T(8,128)}), f32[2,2,4,8,128]{4,3,2,1,0:T(8,128)}) %reduce-scatter.3.cloned.1.call-update) | async-done | bytes 65552 | tf_op jit(solution)/shard_map/reduce_scatter | solution.py:42
  98.4 1.6 fusion.22
  100.0 1.1 copy.25
  101.2 0.0 copy-start.2
  101.2 0.0 reduce-scatter.5.cloned.1.call-update
  101.2 0.7 copy-done.2
  101.9 0.2 fusion.24
  102.1 372.0 %all-reduce.2.cloned.1.call-done = f32[128,128]{0,1:T(8,128)} async-done(((f32[128,128]{0,1:T(8,128)}), f32[128,128]{0,1:T(8,128)}) %all-reduce.2.cloned.1.call-update) | async-done | bytes 65552 | tf_op jit(solution)/shard_map/psum | solution.py:92
  474.1 0.8 broadcast_multiply_fusion
  475.0 0.7 copy.30
  475.7 0.7 slice_bitcast_fusion
  476.4 0.0 copy-done
  476.4 0.9 fusion.3
  477.3 49.3 %all-gather = bf16[2,256,128]{2,1,0:T(8,128)(2,1)S(1)} all-gather(bf16[2,8,128]{2,1,0:T(8,128)(2,1)S(1)} %convert_element_type.44), channel_id=2, replica_groups=mesh['gx'=16,'gy'=32] {'gy'}, dimensions={1}, use_global_device_ids=true | all-gather | bytes 135168 | tf_op jit(solution)/shard_map/all_gather | solution.py:68
  526.7 0.3 convolution_bitcast_fusion.3
  527.0 38.4 %all_gather.7 = f32[32,4,8,128]{3,2,1,0:T(8,128)S(1)} all-gather(f32[2,4,8,128]{3,2,1,0:T(8,128)S(1)} %copy.27), channel_id=1, replica_groups=mesh['gx'=16,'gy'=32] {'gx'}, dimensions={0}, use_global_device_ids=true | all-gather | bytes 557056 | tf_op jit(solution)/shard_map/all_gather | solution.py:75
  565.4 0.7 fusion.5
  566.1 1.1 fusion.2
  567.2 0.9 fusion.1
  (6 shorter events, 0.0 us)
Async XLA Ops:
  8.0 468.4 %copy-start = (bf16[2,1,8,128,128]{4,3,2,1,0:T(8,128)(2,1)S(1)}, bf16[2,1,8,128,128]{4,3,2,1,0:T(8,128)(2,1)}, u32[]{:S(2)}) copy-start(bf16[2,1,8,128,128]{4,3,2,1,0:T(8,128)(2,1)} %param.8) | copy-start | bytes 1572868
  8.0 90.4 %reduce-scatter.3.cloned.1.call-start = ((), (), s32[]{:S(2)}) async-start(), calls=%async_computation.2 | async-start | bytes 1114112 | tf_op jit(solution)/shard_map/reduce_scatter | solution.py:42
  8.1 1.0 copy-start.1
  12.2 461.9 %all-reduce.2.cloned.1.call-start = ((), (), s32[]{:S(2)}) async-start(), calls=%async_computation.4 | async-start | bytes 131072 | tf_op jit(solution)/shard_map/psum | solution.py:92
  13.2 462.5 %reduce-scatter.5.cloned.1.call-start = ((), (), s32[]{:S(2)}) async-start(), calls=%async_computation.3 | async-start | bytes 540672 | tf_op jit(solution)/shard_map/reduce_scatter | solution.py:49
  101.2 0.8 copy-start.2
Sparse Core Ops, SparseCore 0:
  12.4 86.0 reduce-scatter.2
  103.3 117.7 reduce-scatter.4
Sparse Core Ops, SparseCore 1:
  18.8 455.3 all-reduce.1
where the time goes:
time: 578 us; the launch traced here: 576 us
  waiting for transfers between devices  457 us (79%)
  blocking collectives  87.8 us (15%)
  between operations  15.6 us (3%)
  matrix products  6.95 us (1%)
    psum x1, waiting for transfers between devices, on_device(): lax.psum(local_sum, ('gx', 'gy')) / math.sqrt(length_x * length_y * cells_z)  372 us
    reduce_scatter x1, waiting for transfers between devices, on_device(): lax.psum_scatter(jnp.einsum('ai,fijch->afjch', table_rows, z_modes, preci...  85.2 us
    all_gather x1, blocking collectives, on_device(): lax.all_gather(back_modes, 'gy', axis=1, tiled=True).astype(jnp.float32)  49.3 us
    all_gather x1, blocking collectives, on_device(): lax.all_gather(over_second, 'gx', axis=0, tiled=True)  38.4 us
  transfers between devices with their start and end apart: 3, of which 2 were waited for; matrix products, arithmetic and copies ran while one was open for 1% of the time, Pallas kernels for 0%

commit v1 on v0

v1 whole, which is shorter than its diff:
```python
import functools
import math
from types import SimpleNamespace

import jax
import jax.numpy as jnp
import numpy as np
from jax import lax
from jax.experimental import pallas as pl
from jax.experimental.pallas import tpu as pltpu
from jax.sharding import PartitionSpec as P

MESH = pl.DeviceIdType.MESH
F32, BF16 = jnp.float32, jnp.bfloat16

NY, NX, NC = 4, 4, 2


def cas(modes, length):
    index = np.arange(modes)
    freq = np.where(index < modes // 2, index, length - modes + index)
    phase = freq[:, None] * np.arange(length)[None, :] % length
    angle = phase * (2.0 * math.pi / length)
    return (np.cos(angle) + np.sin(angle)) / math.sqrt(length)


def make_tables(s):
    fx = cas(2 * s.gx, 8 * s.gx)
    fy = cas(s.gy, 4 * s.gy)
    e = np.arange(2)
    jj, ii = np.arange(4), np.arange(8)
    cy, cx, cc, cj, ci = np.meshgrid(
        np.arange(NY), np.arange(NX), np.arange(NC), jj, ii, indexing="ij"
    )
    cy, cx, cc, cj, ci = (v.reshape(-1) for v in (cy, cx, cc, cj, ci))
    half = NY // NC
    xt = np.zeros((s.zl, NC, s.zl, half * 2, s.cells))
    for zl in range(s.zl):
        cell_i = 8 * (s.zl * cy + zl) + ci
        for c in range(NC):
            for zd in range(s.zl):
                for y2 in range(half):
                    a = 2 * (s.zl * (half * c + y2) + zd) + e
                    xt[zl, c, zd, y2 * 2 : y2 * 2 + 2] = fx[a][:, cell_i]
    yt = np.zeros((s.zh, s.zh, NX * NC, s.cells))
    xs, cs = (v.reshape(-1) for v in np.meshgrid(np.arange(NX), np.arange(NC), indexing="ij"))
    for zh in range(s.zh):
        cell_j = 4 * ((s.zh * cx + zh) * NC + cc) + cj
        for zd in range(s.zh):
            b = (xs * s.zh + zd) * NC + cs
            yt[zh, zd] = fy[b][:, cell_j]
    mh, ml, me, mx, mc = (
        v.reshape(-1)
        for v in np.meshgrid(
            np.arange(s.zh), np.arange(s.zl), e, np.arange(NX), np.arange(NC), indexing="ij"
        )
    )
    at = np.zeros((s.zl, NY, NY, 8, mh.size))
    for zl in range(s.zl):
        for q in range(NY):
            a = 2 * (s.zl * q + ml) + me
            for y in range(NY):
                at[zl, q, y] = fx[a][:, 8 * (s.zl * y + zl) + ii].T
    bt = np.zeros((s.zh, NX * NC, 4, mh.size))
    b = (mx * s.zh + mh) * NC + mc
    for zh in range(s.zh):
        for k in range(NX * NC):
            bt[zh, k] = fy[b][:, 4 * ((xs[k] * s.zh + zh) * NC + cs[k]) + jj].T
    return [jnp.asarray(v, F32) for v in (xt, yt, at, bt)]


def split(v):
    high = v.astype(BF16)
    return high, (v - high.astype(F32)).astype(BF16)


def kernel(s, inp, pre, cot, w, skw, xt, yt, at, bt, gi, gs, gk, r):
    gx, gy = lax.axis_index("gx"), lax.axis_index("gy")
    y, zl = gx // s.zl, gx % s.zl
    c, zh, x = gy % NC, (gy // NC) % s.zh, gy // (NC * s.zh)
    plane = (y * NX + x) * NC + c
    z = zh * s.zl + zl
    NP, NXC, NZ, NK = NY * NX * NC, NX * NC, s.zl * s.zh, s.nk
    half = NY // NC

    def at_plane(dy, dx, dc):
        yy, xx, cc = (y + dy) % NY, (x + dx) % NX, (c + dc) % NC
        return yy, xx, cc, (yy * s.zl + zl, (xx * s.zh + zh) * NC + cc)

    def at_z(dz):
        zz = (z + dz) % NZ
        return zz, (y * s.zl + zz % s.zl, (x * s.zh + zz // s.zl) * NC + c)

    def hops(d, n):
        return min(d, n - d)

    plane_steps = sorted(
        (
            (dy, dx, dc)
            for dy in range(NY)
            for dx in range(NX)
            for dc in range(NC)
            if dy + dx + dc > 0
        ),
        key=lambda t: -(hops(t[0], NY) + hops(t[1], NX)),
    )
    z_steps = sorted(range(1, NZ), key=lambda d: -hops(d, NZ))

    def send(src, dst, name, device):
        pltpu.make_async_remote_copy(
            src_ref=src,
            dst_ref=dst,
            send_sem=r.send.at[s.phase[name]],
            recv_sem=r.recv.at[s.phase[name]],
            device_id=device,
            device_id_type=MESH,
        ).start()

    def wait(ref, count, name, sems):
        part = ref.at[pl.ds(0, count)]
        pltpu.make_async_copy(part, part, sems.at[s.phase[name]]).wait()

    loads = [
        pltpu.make_async_copy(src, dst, r.local.at[n])
        for n, (src, dst) in enumerate(
            (
                (pre, r.pre),
                (cot, r.cot),
                (inp, r.inp),
                (skw, r.skw),
                (xt.at[zl, c], r.xt),
                (yt.at[zh], r.yt),
                (at.at[zl, y], r.at),
                (bt.at[zh], r.bt),
                (w, r.w),
            )
        )
    ]
    for copy in loads:
        copy.start()

    barrier = pltpu.get_barrier_semaphore()
    for step in plane_steps:
        pl.semaphore_signal(barrier, inc=1, device_id=at_plane(*step)[3], device_id_type=MESH)
    for dz in z_steps:
        pl.semaphore_signal(barrier, inc=1, device_id=at_z(dz)[1], device_id_type=MESH)

    for n in range(3):
        loads[n].wait()
    rows = 32 * NK
    p = r.pre[...].astype(F32).reshape(rows, 128)
    slope = 0.5 * (1.0 + lax.erf(p * (1.0 / math.sqrt(2.0)))) + p * jnp.exp(-0.5 * p * p) * (
        1.0 / math.sqrt(2.0 * math.pi)
    )
    grad = (r.cot[...].astype(F32).reshape(rows, 128) * slope).astype(BF16)
    r.grad[...] = grad
    r.fields[1] = grad.astype(F32)
    r.fields[0] = r.inp[...].astype(F32).reshape(rows, 128)
    for f in range(2):
        for k in range(NK):
            for j in range(0, 4, 2):
                pair = [
                    r.fields[f, pl.ds((j + o) * NK + k, 8, stride=4 * NK), :] for o in range(2)
                ]
                r.blocks[f * NK + k, pl.ds(j * 8, 16), :] = jnp.concatenate(pair, axis=0).astype(BF16)

    pl.semaphore_wait(barrier, len(plane_steps) + len(z_steps))

    for step in plane_steps:
        yy, xx, _, device = at_plane(*step)
        send(r.blocks.at[yy * NX + xx], r.slab.at[plane], "A", device)
    r.slab[plane] = r.blocks[y * NX + x]

    local = lax.dot_general(
        r.inp[...].astype(F32).reshape(rows, 128).astype(BF16),
        r.grad[...],
        (((0,), (0,)), ((), ())),
        preferred_element_type=F32,
    )
    rk = 128 // NP
    for n in range(NP):
        r.skip_a[n] = local[n * rk : (n + 1) * rk]
    for step in plane_steps:
        yy, xx, cc, device = at_plane(*step)
        send(r.skip_a.at[(yy * NX + xx) * NC + cc], r.skip_b.at[plane], "SA", device)
    r.skip_b[plane] = r.skip_a[plane]

    loads[4].wait()
    loads[5].wait()

    @pl.loop(0, NZ)
    def _(zd):
        yv = r.yt[zd // s.zl]
        xv = r.xt[zd % s.zl]
        for y2 in range(half):
            prod = jnp.concatenate(
                [xv[y2 * 2 + e : y2 * 2 + e + 1] * yv for e in range(2)], axis=0
            )
            high, low = split(prod)
            r.th[zd, pl.ds(y2 * 2 * NXC, 2 * NXC), :] = high
            r.tl[zd, pl.ds(y2 * 2 * NXC, 2 * NXC), :] = low

    wait(r.slab, NP - 1, "A", r.recv)
    slab = r.slab[...].reshape(s.cells, 128)
    nm = NZ * half * 2 * NXC
    parts = jnp.dot(r.th[...].reshape(nm, s.cells), slab, preferred_element_type=F32) + jnp.dot(
        r.tl[...].reshape(nm, s.cells), slab, preferred_element_type=F32
    )
    r.parts[...] = parts.astype(BF16).reshape(NZ, half * 2 * NXC, 128)
    for dz in z_steps:
        zz, device = at_z(dz)
        send(r.parts.at[zz], r.sums.at[z], "B", device)
    r.sums[z] = r.parts[z]

    loads[3].wait()
    r.skip[...] = lax.dot_general(
        r.grad[...], r.skw[...], (((1,), (1,)), ((), ())), preferred_element_type=F32
    )
    wait(r.skip_b, NP - 1, "SA", r.recv)
    r.skip_c[...] = jnp.sum(r.skip_b[...], axis=0)
    for dz in z_steps:
        zz, device = at_z(dz)
        send(r.skip_c, r.skip_d.at[z], "SB", device)
    r.skip_d[z] = r.skip_c[...]
    loads[6].wait()
    loads[7].wait()

    @pl.loop(0, NP)
    def _(n):
        av = r.at[n // NXC]
        bv = r.bt[n % NXC]
        for j in range(0, 4, 2):
            high, low = split(
                jnp.concatenate([av * bv[j + o : j + o + 1] for o in range(2)], axis=0)
            )
            r.uh[n, pl.ds(j * 8, 16), :] = high
            r.ul[n, pl.ds(j * 8, 16), :] = low

    wait(r.sums, NZ - 1, "B", r.recv)
    modes = jnp.sum(r.sums[...].astype(F32), axis=0)
    for y2 in range(half):
        for e in range(2):
            for k in range(NXC):
                row = (y2 * 2 + e) * NXC + k
                r.own_a[y2 * NXC + k, e : e + 1, :] = modes[row : row + 1]
    chip = y * NX + x
    mine = y // half == c
    for y2 in range(half):
        for k in range(NXC):
            yy = half * c + y2
            xx, cc = (x + k // NC) % NX, (c + k % NC) % NC
            device = (yy * s.zl + zl, (xx * s.zh + zh) * NC + cc)

            def go(yy=yy, xx=xx, cc=cc, device=device, y2=y2):
                send(r.own_a.at[y2 * NXC + xx * NC + cc], r.own_b.at[chip], "C", device)

            if k == 0:
                pl.when(yy != y)(go)
            else:
                go()

    @pl.when(mine)
    def _():
        r.own_b[chip] = r.own_a[(y % half) * NXC + x * NC + c]
        wait(r.own_b, NY * NX - 1, "C", r.recv)
        wait(r.own_a, half * NXC - 1, "C", r.send)

    @pl.when(jnp.logical_not(mine))
    def _():
        wait(r.own_b, NY * NX, "C", r.recv)
        wait(r.own_a, half * NXC, "C", r.send)

    for f in range(2):
        vals = [r.own_b[f * NK + k] for k in range(NK)]
        for m in range(NK):
            total = vals[0] * s.fz[m][0]
            for k in range(1, NK):
                total += vals[k] * s.fz[m][k]
            r.modes[f, 2 * m : 2 * m + 2, :] = total
    loads[8].wait()
    gm = r.modes[1]
    high, low = split(gm)
    lhs = jnp.concatenate([high, low], axis=0)
    nr = 2 * NK
    for m in range(NK):
        for e in range(2):
            d = lax.dot_general(
                lhs, r.w[e, 0, m], (((1,), (1,)), ((), ())), preferred_element_type=F32
            )
            row = 2 * m + e
            back = d[row : row + 1] + d[nr + row : nr + row + 1]
            r.back_a[m, e : e + 1, :] = back.astype(BF16).astype(F32)

    xc = x * NC + c
    for dy, dx, dc in plane_steps:
        if dy:
            continue
        xx, cc = (x + dx) % NX, (c + dc) % NC
        device = (gx, (xx * s.zh + zh) * NC + cc)
        send(r.back_a.at[xx * NC + cc], r.back_b.at[xc], "D", device)
    r.back_b[xc] = r.back_a[xc]

    im = jnp.transpose(r.modes[0], (1, 0))

    def outer(lo, hi):
        for row in range(lo, hi):
            r.gs[row % 2, 0, row // 2] = (im[:, row : row + 1] * gm[row : row + 1]).astype(BF16)

    outer(0, nr // 2)

    wait(r.back_b, NXC - 1, "D", r.recv)
    block = jnp.concatenate([r.back_b[:, e, :] for e in range(2)], axis=0).astype(BF16)
    r.gather_a[...] = block
    r.gather_b[z] = block
    for dz in z_steps:
        zz, device = at_z(dz)
        send(r.gather_a, r.gather_b.at[z], "E", device)
    outer(nr // 2, nr)
    out = pltpu.make_async_copy(r.gs, gs, r.local.at[9])
    out.start()

    wait(r.skip_d, NZ - 1, "SB", r.recv)
    r.skip_e[...] = jnp.sum(r.skip_d[...], axis=0) * s.scale
    for step in plane_steps:
        device = at_plane(*step)[3]
        send(r.skip_e, r.skip_f.at[plane], "SC", device)
    r.skip_f[plane] = r.skip_e[...]

    wait(r.gather_b, NZ - 1, "E", r.recv)
    gathered = r.gather_b[...].reshape(NZ * 2 * NXC, 128)
    cells = jnp.dot(
        r.uh[...].reshape(s.cells, NZ * 2 * NXC), gathered, preferred_element_type=F32
    ) + jnp.dot(r.ul[...].reshape(s.cells, NZ * 2 * NXC), gathered, preferred_element_type=F32)
    r.cells_a[...] = cells.astype(BF16).reshape(NP, 32, 128)
    for step in plane_steps:
        yy, xx, cc, device = at_plane(*step)
        send(r.cells_a.at[(yy * NX + xx) * NC + cc], r.cells_b.at[plane], "F", device)
    r.cells_b[plane] = r.cells_a[plane]

    wait(r.skip_f, NP - 1, "SC", r.recv)
    gk[...] = r.skip_f[...]

    wait(r.cells_b, NP - 1, "F", r.recv)
    vals = []
    for m in range(NK):
        total = r.cells_b[m].astype(F32)
        for q in range(1, NY):
            total += r.cells_b[q * NXC + m].astype(F32)
        vals.append(total)
    for k in range(NK):
        total = vals[0] * s.fz[0][k]
        for m in range(1, NK):
            total += vals[m] * s.fz[m][k]
        for j in range(4):
            r.fields[0, pl.ds(j * NK + k, 8, stride=4 * NK), :] = total[j * 8 : j * 8 + 8]
    gi[...] = (r.fields[0] + r.skip[...]).astype(BF16).reshape(gi.shape)

    for ref, count, name in (
        (r.slab, NP - 1, "A"),
        (r.skip_a, NP - 1, "SA"),
        (r.sums, NZ - 1, "B"),
        (r.skip_d, NZ - 1, "SB"),
        (r.back_b, NXC - 1, "D"),
        (r.gather_b, NZ - 1, "E"),
        (r.skip_f, NP - 1, "SC"),
        (r.cells_b, NP - 1, "F"),
    ):
        wait(ref, count, name, r.send)
    out.wait()


def solution(mesh):
    def on_device(inputs, preact, cotangent, spectral_w, skip_w):
        nk = inputs.shape[2]
        gx, gy = mesh.shape["gx"], mesh.shape["gy"]
        zl, zh = gx // NY, gy // (NX * NC)
        nz, np_, half, nxc = zl * zh, NY * NX * NC, NY // NC, NX * NC
        names = ("A", "SA", "B", "SB", "C", "D", "E", "SC", "F")
        table = cas(nk, nk)
        s = SimpleNamespace(
            gx=gx,
            gy=gy,
            zl=zl,
            zh=zh,
            nk=nk,
            cells=np_ * 32,
            fz=[[float(v) for v in row] for row in table],
            scale=1.0 / math.sqrt(gx * 8 * gy * 4 * nk),
            phase={name: n for n, name in enumerate(names)},
        )
        tables = make_tables(s)
        rk = 128 // np_
        V = pltpu.VMEM
        scratch = dict(
            inp=V(inputs.shape, BF16),
            pre=V(inputs.shape, BF16),
            cot=V(inputs.shape, BF16),
            skw=V((128, 128), BF16),
            w=V(spectral_w.shape, BF16),
            gs=V(spectral_w.shape, BF16),
            xt=V(tables[0].shape[2:], F32),
            yt=V(tables[1].shape[1:], F32),
            at=V(tables[2].shape[2:], F32),
            bt=V(tables[3].shape[1:], F32),
            fields=V((2, 32 * nk, 128), F32),
            grad=V((32 * nk, 128), BF16),
            skip=V((32 * nk, 128), F32),
            blocks=V((2 * nk, 32, 128), BF16),
            slab=V((np_, 32, 128), BF16),
            th=V((nz, half * 2 * nxc, s.cells), BF16),
            tl=V((nz, half * 2 * nxc, s.cells), BF16),
            parts=V((nz, half * 2 * nxc, 128), BF16),
            sums=V((nz, half * 2 * nxc, 128), BF16),
            own_a=V((half * nxc, 2, 128), F32),
            own_b=V((NY * NX, 2, 128), F32),
            modes=V((2, 2 * nk, 128), F32),
            back_a=V((nk, 2, 128), F32),
            back_b=V((nxc, 2, 128), F32),
            gather_a=V((2 * nxc, 128), BF16),
            gather_b=V((nz, 2 * nxc, 128), BF16),
            uh=V((np_, 32, nz * 2 * nxc), BF16),
            ul=V((np_, 32, nz * 2 * nxc), BF16),
            cells_a=V((np_, 32, 128), BF16),
            cells_b=V((np_, 32, 128), BF16),
            skip_a=V((np_, rk, 128), F32),
            skip_b=V((np_, rk, 128), F32),
            skip_c=V((rk, 128), F32),
            skip_d=V((nz, rk, 128), F32),
            skip_e=V((rk, 128), F32),
            skip_f=V((np_, rk, 128), F32),
            send=pltpu.SemaphoreType.DMA((len(names),)),
            recv=pltpu.SemaphoreType.DMA((len(names),)),
            local=pltpu.SemaphoreType.DMA((10,)),
        )

        def body(*refs):
            kernel(s, *refs[:12], SimpleNamespace(**dict(zip(scratch, refs[12:]))))

        any_space = pl.BlockSpec(memory_space=pl.ANY)
        vmem = pl.BlockSpec(memory_space=pltpu.VMEM)
        gi, gs, gk = pl.pallas_call(
            body,
            out_shape=(
                jax.ShapeDtypeStruct(inputs.shape, BF16),
                jax.ShapeDtypeStruct(spectral_w.shape, BF16),
                jax.ShapeDtypeStruct((np_, rk, 128), F32),
            ),
            in_specs=[any_space] * 9,
            out_specs=(vmem, any_space, vmem),
            scratch_shapes=list(scratch.values()),
            compiler_params=pltpu.CompilerParams(
                collective_id=0, has_side_effects=True, vmem_limit_bytes=32 << 20
            ),
            name="layer",
        )(inputs, preact, cotangent, spectral_w, skip_w, *tables)
        return gi, gs, gk.reshape(128, 128)

    cells = P("gx", "gy", None, None)
    weights = P("gx", "gy", None, None, None)
    return jax.shard_map(
        on_device,
        mesh=mesh,
        in_specs=(cells, cells, cells, weights, P()),
        out_specs=(cells, weights, P()),
        check_vma=False,
    )
```

time: 578 us -> 68.2 us (0.12)
  waiting for transfers between devices: 457 us -> 0 us
  blocking collectives: 87.8 us -> 0 us
  Pallas kernels: 0 us -> 56.6 us
  between operations: 15.6 us -> 0.66 us
  matrix products: 6.95 us -> 0 us
    psum x1 -> x0, waiting for transfers between devices: 372 us -> none  [on_device(): lax.psum(local_sum, ('gx', 'gy')) / math.sqrt(length_x * length_y * cells_z)]
    all_gather x2 -> x0, blocking collectives: 87.8 us -> none  [the longest x1 49.3 us: on_device(): lax.all_gather(back_modes, 'gy', axis=1, tiled=True).astype(jnp.float32)]
    reduce_scatter x2 -> x0, waiting for transfers between devices: 85.2 us -> none  [the longest x1 85.2 us: on_device(): lax.psum_scatter(jnp.einsum('ai,fijch->afjch', table_rows, z_modes, preci...]
    pallas_call x0 -> x1, Pallas kernels: none -> 56.6 us  [on_device(): pl.pallas_call(body, out_shape=(jax.ShapeDtypeStruct(inputs.shape, BF16),...]
    unnamed x7 -> x21, local copies, waits for them, and re-layouts: 1.48 us -> 10.4 us
    dot_general x9 -> x0, matrix products: 6.95 us -> none  [the longest x1 1.59 us: on_device(): jnp.einsum('bj,afjch->bafch', table_rows, part_x, precision=highest)]
  transfers between devices with their start and end apart: 3 -> 0, of which waited for: 2 -> 0; matrix products, arithmetic and copies ran while one was open for 1% -> 0% of each run, Pallas kernels for 0% -> 0%
where the time goes in v1:
time: 68.2 us; the launch traced here: 67.6 us
  Pallas kernels  56.6 us (83%)
  local copies, waits for them, and re-layouts  10.4 us (15%)
    pallas_call x1, Pallas kernels, on_device(): pl.pallas_call(body, out_shape=(jax.ShapeDtypeStruct(inputs.shape, BF16),...  56.6 us
    unnamed x21, local copies, waits for them, and re-layouts  10.4 us

profile of v1, /device:TPU:1, one launch (start us, length us, event | category | flops | bytes accessed | tf_op | source)
XLA Modules:
  0.0 67.6 jit_solution(13596431685396430374)
XLA Ops:
  0.6 0.0 copy-start
  0.6 1.0 %copy-done = bf16[2,1,8,128,128]{4,3,2,1,0:T(8,128)(2,1)S(1)} copy-done((bf16[2,1,8,128,128]{4,3,2,1,0:T(8,128)(2,1)S(1)}, bf16[2,1,8,128,128]{4,3,2,1,0:T(8,128)(2,1)}, u32[]{:S(2)}) %copy-start) | copy-done | bytes 524312
  1.7 0.0 copy-start.1
  1.7 1.0 %copy-done.1 = f32[4,4,4,8,256]{4,3,2,1,0:T(8,128)S(1)} copy-done((f32[4,4,4,8,256]{4,3,2,1,0:T(8,128)S(1)}, f32[4,4,4,8,256]{4,3,2,1,0:T(8,128)}, u32[]{:S(2)}) %copy-start.1) | copy-done | bytes 524312
  2.7 0.0 copy-start.2
  2.7 1.0 %copy-done.2 = f32[4,4,8,1024]{3,2,1,0:T(8,128)S(1)} copy-done((f32[4,4,8,1024]{3,2,1,0:T(8,128)S(1)}, f32[4,4,8,1024]{3,2,1,0:T(8,128)}, u32[]{:S(2)}) %copy-start.2) | copy-done | bytes 524312
  3.8 0.0 copy-start.3
  3.8 1.0 %copy-done.3 = f32[4,2,4,4,1024]{4,3,2,1,0:T(4,128)S(1)} copy-done((f32[4,2,4,4,1024]{4,3,2,1,0:T(4,128)S(1)}, f32[4,2,4,4,1024]{4,3,2,1,0:T(4,128)}, u32[]{:S(2)}) %copy-start.3) | copy-done | bytes 524312
  4.8 0.0 copy-start.4
  4.8 0.9 %copy-done.4 = f32[4,8,4,256]{3,2,1,0:T(4,128)S(1)} copy-done((f32[4,8,4,256]{3,2,1,0:T(4,128)S(1)}, f32[4,8,4,256]{3,2,1,0:T(4,128)}, u32[]{:S(2)}) %copy-start.4) | copy-done | bytes 131096
  5.7 0.0 copy-start.5
  5.7 0.8 %copy-done.5 = bf16[8,4,8,128]{3,2,1,0:T(8,128)(2,1)S(1)} copy-done((bf16[8,4,8,128]{3,2,1,0:T(8,128)(2,1)S(1)}, bf16[8,4,8,128]{3,2,1,0:T(8,128)(2,1)}, u32[]{:S(2)}) %copy-start.5) | copy-done | bytes 65560
  6.5 0.0 copy-start.6
  6.5 0.8 %copy-done.6 = bf16[8,4,8,128]{3,2,1,0:T(8,128)(2,1)S(1)} copy-done((bf16[8,4,8,128]{3,2,1,0:T(8,128)(2,1)S(1)}, bf16[8,4,8,128]{3,2,1,0:T(8,128)(2,1)}, u32[]{:S(2)}) %copy-start.6) | copy-done | bytes 65560
  7.4 0.0 copy-start.7
  7.4 0.8 %copy-done.7 = bf16[8,4,8,128]{3,2,1,0:T(8,128)(2,1)S(1)} copy-done((bf16[8,4,8,128]{3,2,1,0:T(8,128)(2,1)S(1)}, bf16[8,4,8,128]{3,2,1,0:T(8,128)(2,1)}, u32[]{:S(2)}) %copy-start.7) | copy-done | bytes 65560
  8.2 0.0 copy-start.8
  8.2 0.8 %copy-done.8 = bf16[128,128]{1,0:T(8,128)(2,1)S(1)} copy-done((bf16[128,128]{1,0:T(8,128)(2,1)S(1)}, bf16[128,128]{1,0:T(8,128)(2,1)}, u32[]{:S(2)}) %copy-start.8) | copy-done | bytes 32792
  9.0 56.6 %layer.1 = (bf16[8,4,8,128]{3,2,1,0:T(8,128)(2,1)S(1)}, bf16[2,1,8,128,128]{4,3,2,1,0:T(8,128)(2,1)S(1)}, f32[32,4,128]{2,1,0:T(4,128)S(1)}) custom-call(bf16[8,4,8,128]{3,2,1,0:T(8,128)(2,1)S(1)} %copy-done.5, bf16[8,4,8,128]{3,2,1,0:T(8,128)(2,1)S(1)} %copy-done.6, bf16[8,4,8,128]{3,2,1,0:T(8,128)(2,1)S(1)} %copy-done.7, ...), custom_call_target="tpu_custom_call" | custom-call | tf_op jit(solution)/shard_map/layer/pallas_call | solution.py:441
  65.6 0.6 copy.15
  66.2 0.8 %copy.16 = bf16[2,1,8,128,128]{4,3,2,1,0:T(8,128)(2,1)} copy(bf16[2,1,8,128,128]{4,3,2,1,0:T(8,128)(2,1)S(1)} %get-tuple-element.13) | data formatting | bytes 1048576
  67.0 0.6 copy.17
Async XLA Ops:
  0.6 1.0 %copy-start = (bf16[2,1,8,128,128]{4,3,2,1,0:T(8,128)(2,1)S(1)}, bf16[2,1,8,128,128]{4,3,2,1,0:T(8,128)(2,1)}, u32[]{:S(2)}) copy-start(bf16[2,1,8,128,128]{4,3,2,1,0:T(8,128)(2,1)} %refs_3_.1) | copy-start | bytes 1572868
  1.7 1.0 %copy-start.1 = (f32[4,4,4,8,256]{4,3,2,1,0:T(8,128)S(1)}, f32[4,4,4,8,256]{4,3,2,1,0:T(8,128)}, u32[]{:S(2)}) copy-start(f32[4,4,4,8,256]{4,3,2,1,0:T(8,128)} %constant.10.clone.refs_7_) | copy-start | bytes 1572868
  2.7 1.0 %copy-start.2 = (f32[4,4,8,1024]{3,2,1,0:T(8,128)S(1)}, f32[4,4,8,1024]{3,2,1,0:T(8,128)}, u32[]{:S(2)}) copy-start(f32[4,4,8,1024]{3,2,1,0:T(8,128)} %constant.9.clone.refs_6_) | copy-start | bytes 1572868
  3.8 1.0 %copy-start.3 = (f32[4,2,4,4,1024]{4,3,2,1,0:T(4,128)S(1)}, f32[4,2,4,4,1024]{4,3,2,1,0:T(4,128)}, u32[]{:S(2)}) copy-start(f32[4,2,4,4,1024]{4,3,2,1,0:T(4,128)} %constant.8.clone.refs_5_) | copy-start | bytes 1572868
  4.8 0.9 %copy-start.4 = (f32[4,8,4,256]{3,2,1,0:T(4,128)S(1)}, f32[4,8,4,256]{3,2,1,0:T(4,128)}, u32[]{:S(2)}) copy-start(f32[4,8,4,256]{3,2,1,0:T(4,128)} %constant.11.clone.refs_8_) | copy-start | bytes 393220
  5.7 0.8 %copy-start.5 = (bf16[8,4,8,128]{3,2,1,0:T(8,128)(2,1)S(1)}, bf16[8,4,8,128]{3,2,1,0:T(8,128)(2,1)}, u32[]{:S(2)}) copy-start(bf16[8,4,8,128]{3,2,1,0:T(8,128)(2,1)} %refs_0_.1) | copy-start | bytes 196612
  6.5 0.8 %copy-start.6 = (bf16[8,4,8,128]{3,2,1,0:T(8,128)(2,1)S(1)}, bf16[8,4,8,128]{3,2,1,0:T(8,128)(2,1)}, u32[]{:S(2)}) copy-start(bf16[8,4,8,128]{3,2,1,0:T(8,128)(2,1)} %refs_1_.1) | copy-start | bytes 196612
  7.4 0.8 %copy-start.7 = (bf16[8,4,8,128]{3,2,1,0:T(8,128)(2,1)S(1)}, bf16[8,4,8,128]{3,2,1,0:T(8,128)(2,1)}, u32[]{:S(2)}) copy-start(bf16[8,4,8,128]{3,2,1,0:T(8,128)(2,1)} %refs_2_.1) | copy-start | bytes 196612
  8.2 0.8 %copy-start.8 = (bf16[128,128]{1,0:T(8,128)(2,1)S(1)}, bf16[128,128]{1,0:T(8,128)(2,1)}, u32[]{:S(2)}) copy-start(bf16[128,128]{1,0:T(8,128)(2,1)} %refs_4_.1) | copy-start | bytes 98308

commit v2 on v1

--- a/solution.py
+++ b/solution.py
@@ -180,11 +180,6 @@
     rk = 128 // NP
     for n in range(NP):
         r.skip_a[n] = local[n * rk : (n + 1) * rk]
-    for step in plane_steps:
-        yy, xx, cc, device = at_plane(*step)
-        send(r.skip_a.at[(yy * NX + xx) * NC + cc], r.skip_b.at[plane], "SA", device)
-    r.skip_b[plane] = r.skip_a[plane]
-
     loads[4].wait()
     loads[5].wait()
 
@@ -212,16 +207,14 @@
         send(r.parts.at[zz], r.sums.at[z], "B", device)
     r.sums[z] = r.parts[z]
 
+    for step in plane_steps:
+        yy, xx, cc, device = at_plane(*step)
+        send(r.skip_a.at[(yy * NX + xx) * NC + cc], r.skip_b.at[plane], "SA", device)
+    r.skip_b[plane] = r.skip_a[plane]
     loads[3].wait()
     r.skip[...] = lax.dot_general(
         r.grad[...], r.skw[...], (((1,), (1,)), ((), ())), preferred_element_type=F32
     )
-    wait(r.skip_b, NP - 1, "SA", r.recv)
-    r.skip_c[...] = jnp.sum(r.skip_b[...], axis=0)
-    for dz in z_steps:
-        zz, device = at_z(dz)
-        send(r.skip_c, r.skip_d.at[z], "SB", device)
-    r.skip_d[z] = r.skip_c[...]
     loads[6].wait()
     loads[7].wait()
 
@@ -258,6 +251,13 @@
                 pl.when(yy != y)(go)
             else:
                 go()
+
+    wait(r.skip_b, NP - 1, "SA", r.recv)
+    r.skip_c[...] = jnp.sum(r.skip_b[...], axis=0)
+    for dz in z_steps:
+        zz, device = at_z(dz)
+        send(r.skip_c, r.skip_d.at[z], "SB", device)
+    r.skip_d[z] = r.skip_c[...]
 
     @pl.when(mine)
     def _():
@@ -449,7 +449,7 @@
             out_specs=(vmem, any_space, vmem),
             scratch_shapes=list(scratch.values()),
             compiler_params=pltpu.CompilerParams(
-                collective_id=0, has_side_effects=True, vmem_limit_bytes=32 << 20
+                collective_id=0, has_side_effects=True
             ),
             name="layer",
         )(inputs, preact, cotangent, spectral_w, skip_w, *tables)

time: 68.2 us -> 60.4 us (0.89)
  local copies, waits for them, and re-layouts: 10.4 us -> 4.02 us
  Pallas kernels: 56.6 us -> 55.6 us
    unnamed x21 -> x5, local copies, waits for them, and re-layouts: 10.4 us -> 4.02 us
    pallas_call x1, Pallas kernels: 56.6 us -> 55.6 us  [on_device(): pl.pallas_call(body, out_shape=(jax.ShapeDtypeStruct(inputs.shape, BF16),...]
where the time goes in v2:
time: 60.4 us; the launch traced here: 60.2 us
  Pallas kernels  55.6 us (92%)
  local copies, waits for them, and re-layouts  4.02 us (7%)
  between operations  0.64 us (1%)
    pallas_call x1, Pallas kernels, on_device(): pl.pallas_call(body, out_shape=(jax.ShapeDtypeStruct(inputs.shape, BF16),...  55.6 us
    unnamed x5, local copies, waits for them, and re-layouts  4.02 us

profile of v2, /device:TPU:1, one launch (start us, length us, event | category | flops | bytes accessed | tf_op | source)
XLA Modules:
  0.0 60.2 jit_solution(14001155055831525478)
XLA Ops:
  0.6 55.6 %layer.1 = (bf16[8,4,8,128]{3,2,1,0:T(8,128)(2,1)}, bf16[2,1,8,128,128]{4,3,2,1,0:T(8,128)(2,1)}, f32[32,4,128]{2,1,0:T(4,128)}) custom-call(bf16[8,4,8,128]{3,2,1,0:T(8,128)(2,1)} %refs_0_.1, bf16[8,4,8,128]{3,2,1,0:T(8,128)(2,1)} %refs_1_.1, bf16[8,4,8,128]{3,2,1,0:T(8,128)(2,1)} %refs_2_.1, bf16[2,1,8,128,128]{4,3,2,1,0:T(8,128)(2,1)} %refs_3_.1, ...), custom_call_target="tpu_custom_call" | custom-call | tf_op jit(solution)/shard_map/layer/pallas_call | solution.py:441
  56.2 1.5 %copy.15 = bf16[8,4,8,128]{3,2,1,0:T(8,128)(2,1)} copy(bf16[8,4,8,128]{3,2,1,0:T(8,128)(2,1)} %get-tuple-element.12) | data formatting | bytes 131072
  57.7 0.0 copy-start
  57.7 1.9 %copy.16 = bf16[2,1,8,128,128]{4,3,2,1,0:T(8,128)(2,1)} copy(bf16[2,1,8,128,128]{4,3,2,1,0:T(8,128)(2,1)} %get-tuple-element.13) | data formatting | bytes 1048576
  59.6 0.0 copy-done
  59.6 0.6 %copy.17 = f32[128,128]{1,0:T(8,128)} copy(f32[128,128]{1,0:T(8,128)S(1)} %bitcast.1) | data formatting | bytes 131072
Async XLA Ops:
  57.7 1.9 %copy-start = (f32[32,4,128]{2,1,0:T(4,128)S(1)}, f32[32,4,128]{2,1,0:T(4,128)}, u32[]{:S(2)}) copy-start(f32[32,4,128]{2,1,0:T(4,128)} %get-tuple-element.8) | copy-start | bytes 196612

commit v3 on v2

--- a/solution.py
+++ b/solution.py
@@ -120,6 +120,14 @@
         part = ref.at[pl.ds(0, count)]
         pltpu.make_async_copy(part, part, sems.at[s.phase[name]]).wait()
 
+    reach = min(4, NZ // 2)
+    near = [dz for dz in z_steps if hops(dz, NZ) <= reach]
+    barrier = pltpu.get_barrier_semaphore()
+    for step in plane_steps:
+        pl.semaphore_signal(barrier, inc=1, device_id=at_plane(*step)[3], device_id_type=MESH)
+    for dz in near:
+        pl.semaphore_signal(barrier, inc=1, device_id=at_z(dz)[1], device_id_type=MESH)
+
     loads = [
         pltpu.make_async_copy(src, dst, r.local.at[n])
         for n, (src, dst) in enumerate(
@@ -139,12 +147,6 @@
     for copy in loads:
         copy.start()
 
-    barrier = pltpu.get_barrier_semaphore()
-    for step in plane_steps:
-        pl.semaphore_signal(barrier, inc=1, device_id=at_plane(*step)[3], device_id_type=MESH)
-    for dz in z_steps:
-        pl.semaphore_signal(barrier, inc=1, device_id=at_z(dz)[1], device_id_type=MESH)
-
     for n in range(3):
         loads[n].wait()
     rows = 32 * NK
@@ -164,7 +166,10 @@
                 ]
                 r.blocks[f * NK + k, pl.ds(j * 8, 16), :] = jnp.concatenate(pair, axis=0).astype(BF16)
 
-    pl.semaphore_wait(barrier, len(plane_steps) + len(z_steps))
+    pl.semaphore_wait(barrier, len(plane_steps) + len(near))
+    relays = [dz for dz in near if hops(dz, NZ) == reach] if reach < NZ // 2 else []
+    for dz in relays:
+        pl.semaphore_signal(r.far, inc=1, device_id=at_z(dz)[1], device_id_type=MESH)
 
     for step in plane_steps:
         yy, xx, _, device = at_plane(*step)
@@ -183,8 +188,10 @@
     loads[4].wait()
     loads[5].wait()
 
-    @pl.loop(0, NZ)
-    def _(zd):
+    order = z_steps + [0]
+
+    def forward_table(n, dz):
+        zd = (z + dz) % NZ
         yv = r.yt[zd // s.zl]
         xv = r.xt[zd % s.zl]
         for y2 in range(half):
@@ -192,20 +199,26 @@
                 [xv[y2 * 2 + e : y2 * 2 + e + 1] * yv for e in range(2)], axis=0
             )
             high, low = split(prod)
-            r.th[zd, pl.ds(y2 * 2 * NXC, 2 * NXC), :] = high
-            r.tl[zd, pl.ds(y2 * 2 * NXC, 2 * NXC), :] = low
+            r.th[n, pl.ds(y2 * 2 * NXC, 2 * NXC), :] = high
+            r.tl[n, pl.ds(y2 * 2 * NXC, 2 * NXC), :] = low
+
+    for n, dz in enumerate(order):
+        forward_table(n, dz)
 
     wait(r.slab, NP - 1, "A", r.recv)
     slab = r.slab[...].reshape(s.cells, 128)
-    nm = NZ * half * 2 * NXC
-    parts = jnp.dot(r.th[...].reshape(nm, s.cells), slab, preferred_element_type=F32) + jnp.dot(
-        r.tl[...].reshape(nm, s.cells), slab, preferred_element_type=F32
-    )
-    r.parts[...] = parts.astype(BF16).reshape(NZ, half * 2 * NXC, 128)
-    for dz in z_steps:
-        zz, device = at_z(dz)
-        send(r.parts.at[zz], r.sums.at[z], "B", device)
-    r.sums[z] = r.parts[z]
+    if relays:
+        pl.semaphore_wait(r.far, len(relays))
+    chunk = NZ // s.chunks
+    nm = chunk * half * 2 * NXC
+    for g in range(0, NZ, chunk):
+        parts = jnp.dot(
+            r.th[g : g + chunk].reshape(nm, s.cells), slab, preferred_element_type=F32
+        ) + jnp.dot(r.tl[g : g + chunk].reshape(nm, s.cells), slab, preferred_element_type=F32)
+        r.parts[g : g + chunk] = parts.astype(BF16).reshape(chunk, half * 2 * NXC, 128)
+        for n in range(g, min(g + chunk, NZ - 1)):
+            send(r.parts.at[n], r.sums.at[z], "B", at_z(order[n])[1])
+    r.sums[z] = r.parts[NZ - 1]
 
     for step in plane_steps:
         yy, xx, cc, device = at_plane(*step)
@@ -218,9 +231,13 @@
     loads[6].wait()
     loads[7].wait()
 
+    yorder = sorted(range(NY), key=lambda d: -hops(d, NY))
+
     @pl.loop(0, NP)
     def _(n):
-        av = r.at[n // NXC]
+        step = n // NXC
+        dy = sum((jnp.where(step == g, d, 0) for g, d in enumerate(yorder)), 0)
+        av = r.at[(y + dy) % NY]
         bv = r.bt[n % NXC]
         for j in range(0, 4, 2):
             high, low = split(
@@ -328,14 +345,18 @@
 
     wait(r.gather_b, NZ - 1, "E", r.recv)
     gathered = r.gather_b[...].reshape(NZ * 2 * NXC, 128)
-    cells = jnp.dot(
-        r.uh[...].reshape(s.cells, NZ * 2 * NXC), gathered, preferred_element_type=F32
-    ) + jnp.dot(r.ul[...].reshape(s.cells, NZ * 2 * NXC), gathered, preferred_element_type=F32)
-    r.cells_a[...] = cells.astype(BF16).reshape(NP, 32, 128)
-    for step in plane_steps:
-        yy, xx, cc, device = at_plane(*step)
-        send(r.cells_a.at[(yy * NX + xx) * NC + cc], r.cells_b.at[plane], "F", device)
-    r.cells_b[plane] = r.cells_a[plane]
+    nc = NXC * 32
+    for g, dy in enumerate(yorder):
+        part = slice(g * NXC, (g + 1) * NXC)
+        cells = jnp.dot(
+            r.uh[part].reshape(nc, NZ * 2 * NXC), gathered, preferred_element_type=F32
+        ) + jnp.dot(r.ul[part].reshape(nc, NZ * 2 * NXC), gathered, preferred_element_type=F32)
+        r.cells_a[part] = cells.astype(BF16).reshape(NXC, 32, 128)
+        for step in plane_steps:
+            if step[0] == dy:
+                _, xx, cc, device = at_plane(*step)
+                send(r.cells_a.at[g * NXC + xx * NC + cc], r.cells_b.at[plane], "F", device)
+    r.cells_b[plane] = r.cells_a[yorder.index(0) * NXC + xc]
 
     wait(r.skip_f, NP - 1, "SC", r.recv)
     gk[...] = r.skip_f[...]
@@ -384,6 +405,7 @@
             zh=zh,
             nk=nk,
             cells=np_ * 32,
+            chunks=2,
             fz=[[float(v) for v in row] for row in table],
             scale=1.0 / math.sqrt(gx * 8 * gy * 4 * nk),
             phase={name: n for n, name in enumerate(names)},
@@ -431,6 +453,7 @@
             send=pltpu.SemaphoreType.DMA((len(names),)),
             recv=pltpu.SemaphoreType.DMA((len(names),)),
             local=pltpu.SemaphoreType.DMA((10,)),
+            far=pltpu.SemaphoreType.REGULAR,
         )
 
         def body(*refs):
@@ -445,15 +468,37 @@
                 jax.ShapeDtypeStruct(spectral_w.shape, BF16),
                 jax.ShapeDtypeStruct((np_, rk, 128), F32),
             ),
-            in_specs=[any_space] * 9,
+            in_specs=[pl.BlockSpec(memory_space=pltpu.HBM)] * 9,
             out_specs=(vmem, any_space, vmem),
             scratch_shapes=list(scratch.values()),
             compiler_params=pltpu.CompilerParams(
-                collective_id=0, has_side_effects=True
+                collective_id=0, has_side_effects=True, vmem_limit_bytes=16 << 20
             ),
             name="layer",
-        )(inputs, preact, cotangent, spectral_w, skip_w, *tables)
-        return gi, gs, gk.reshape(128, 128)
+        )(
+            *(
+                pltpu.with_memory_space_constraint(v, pltpu.HBM)
+                for v in (inputs, preact, cotangent, spectral_w, skip_w, *tables)
+            )
+        )
+        outs = (gi, gs, gk.reshape(128, 128))
+
+        def store(*refs):
+            copies = [pltpu.make_async_copy(refs[n], refs[3 + n], refs[6].at[n]) for n in range(3)]
+            for copy in copies:
+                copy.start()
+            for copy in copies:
+                copy.wait()
+
+        return pl.pallas_call(
+            store,
+            out_shape=tuple(jax.ShapeDtypeStruct(v.shape, v.dtype) for v in outs),
+            in_specs=[any_space] * 3,
+            out_specs=[pl.BlockSpec(memory_space=pltpu.HBM)] * 3,
+            scratch_shapes=[pltpu.SemaphoreType.DMA((3,))],
+            compiler_params=pltpu.CompilerParams(vmem_limit_bytes=4 << 20),
+            name="store",
+        )(*outs)
 
     cells = P("gx", "gy", None, None)
     weights = P("gx", "gy", None, None, None)

time: 60.4 us -> 52.8 us (0.87)
  local copies, waits for them, and re-layouts: 4.02 us -> 0 us
  Pallas kernels: 55.6 us -> 52 us
    pallas_call x1, Pallas kernels: 55.6 us -> 51.2 us  [on_device(): pl.pallas_call(body, out_shape=(jax.ShapeDtypeStruct(inputs.shape, BF16),...]
    unnamed x5 -> x0, local copies, waits for them, and re-layouts: 4.02 us -> none
    pallas_call x0 -> x1, Pallas kernels: none -> 0.85 us  [on_device(): pl.pallas_call(store, out_shape=tuple((jax.ShapeDtypeStruct(v.shape, v.dt...]
where the time goes in v3:
time: 52.8 us; the launch traced here: 52.6 us
  Pallas kernels  52 us (98%)
  between operations  0.64 us (1%)
    pallas_call x1, Pallas kernels, on_device(): pl.pallas_call(body, out_shape=(jax.ShapeDtypeStruct(inputs.shape, BF16),...  51.2 us

profile of v3, /device:TPU:1, one launch (start us, length us, event | category | flops | bytes accessed | tf_op | source)
XLA Modules:
  0.0 52.6 jit_solution(15244986086925473424)
XLA Ops:
  0.6 51.2 %layer.1 = (bf16[8,4,8,128]{3,2,1,0:T(8,128)(2,1)S(1)}, bf16[2,1,8,128,128]{4,3,2,1,0:T(8,128)(2,1)S(1)}, f32[32,4,128]{2,1,0:T(4,128)S(1)}) custom-call(bf16[8,4,8,128]{3,2,1,0:T(8,128)(2,1)} %refs_0_.1, bf16[8,4,8,128]{3,2,1,0:T(8,128)(2,1)} %refs_1_.1, bf16[8,4,8,128]{3,2,1,0:T(8,128)(2,1)} %refs_2_.1, bf16[2,1,8,128,128]{4,3,2,1,0:T(8,128)(2,1)} %refs_3_.1, ...), custom_call_target="tpu_custom_call" | custom-call | tf_op jit(solution)/shard_map/layer/pallas_call | solution.py:464
  51.8 0.9 %store.1 = (bf16[8,4,8,128]{3,2,1,0:T(8,128)(2,1)}, bf16[2,1,8,128,128]{4,3,2,1,0:T(8,128)(2,1)}, f32[128,128]{1,0:T(8,128)}) custom-call(bf16[8,4,8,128]{3,2,1,0:T(8,128)(2,1)S(1)} %get-tuple-element.6.refs_0_, bf16[2,1,8,128,128]{4,3,2,1,0:T(8,128)(2,1)S(1)} %get-tuple-element.7.refs_1_, f32[128,128]{1,0:T(8,128)S(1)} %bitcast.1), custom_call_target="tpu_custom_call" | custom-call | tf_op jit(solution)/shard_map/store/pallas_call | solution.py:493

commit v4 on v3

--- a/solution.py
+++ b/solution.py
@@ -33,26 +33,23 @@
         np.arange(NY), np.arange(NX), np.arange(NC), jj, ii, indexing="ij"
     )
     cy, cx, cc, cj, ci = (v.reshape(-1) for v in (cy, cx, cc, cj, ci))
-    half = NY // NC
-    xt = np.zeros((s.zl, NC, s.zl, half * 2, s.cells))
+    xt = np.zeros((s.zl, NY, s.zl, 2, s.cells))
     for zl in range(s.zl):
         cell_i = 8 * (s.zl * cy + zl) + ci
-        for c in range(NC):
+        for y in range(NY):
             for zd in range(s.zl):
-                for y2 in range(half):
-                    a = 2 * (s.zl * (half * c + y2) + zd) + e
-                    xt[zl, c, zd, y2 * 2 : y2 * 2 + 2] = fx[a][:, cell_i]
-    yt = np.zeros((s.zh, s.zh, NX * NC, s.cells))
+                xt[zl, y, zd] = fx[2 * (s.zl * y + zd) + e][:, cell_i]
+    yt = np.zeros((s.zh, s.zh, 2 * NX * NC, s.cells))
     xs, cs = (v.reshape(-1) for v in np.meshgrid(np.arange(NX), np.arange(NC), indexing="ij"))
     for zh in range(s.zh):
         cell_j = 4 * ((s.zh * cx + zh) * NC + cc) + cj
         for zd in range(s.zh):
             b = (xs * s.zh + zd) * NC + cs
-            yt[zh, zd] = fy[b][:, cell_j]
-    mh, ml, me, mx, mc = (
+            yt[zh, zd] = np.repeat(fy[b][:, cell_j], 2, axis=0)
+    mh, ml, mx, mc, me = (
         v.reshape(-1)
         for v in np.meshgrid(
-            np.arange(s.zh), np.arange(s.zl), e, np.arange(NX), np.arange(NC), indexing="ij"
+            np.arange(s.zh), np.arange(s.zl), np.arange(NX), np.arange(NC), e, indexing="ij"
         )
     )
     at = np.zeros((s.zl, NY, NY, 8, mh.size))
@@ -81,7 +78,6 @@
     plane = (y * NX + x) * NC + c
     z = zh * s.zl + zl
     NP, NXC, NZ, NK = NY * NX * NC, NX * NC, s.zl * s.zh, s.nk
-    half = NY // NC
 
     def at_plane(dy, dx, dc):
         yy, xx, cc = (y + dy) % NY, (x + dx) % NX, (c + dc) % NC
@@ -136,7 +132,7 @@
                 (cot, r.cot),
                 (inp, r.inp),
                 (skw, r.skw),
-                (xt.at[zl, c], r.xt),
+                (xt.at[zl, y], r.xt),
                 (yt.at[zh], r.yt),
                 (at.at[zl, y], r.at),
                 (bt.at[zh], r.bt),
@@ -147,7 +143,7 @@
     for copy in loads:
         copy.start()
 
-    for n in range(3):
+    for n in range(2):
         loads[n].wait()
     rows = 32 * NK
     p = r.pre[...].astype(F32).reshape(rows, 128)
@@ -157,27 +153,49 @@
     grad = (r.cot[...].astype(F32).reshape(rows, 128) * slope).astype(BF16)
     r.grad[...] = grad
     r.fields[1] = grad.astype(F32)
-    r.fields[0] = r.inp[...].astype(F32).reshape(rows, 128)
-    for f in range(2):
+
+    def make_blocks(f):
         for k in range(NK):
             for j in range(0, 4, 2):
                 pair = [
                     r.fields[f, pl.ds((j + o) * NK + k, 8, stride=4 * NK), :] for o in range(2)
                 ]
-                r.blocks[f * NK + k, pl.ds(j * 8, 16), :] = jnp.concatenate(pair, axis=0).astype(BF16)
+                r.blocks[f, k, pl.ds(j * 8, 16), :] = jnp.concatenate(pair, axis=0).astype(BF16)
+
+    make_blocks(1)
 
     pl.semaphore_wait(barrier, len(plane_steps) + len(near))
     relays = [dz for dz in near if hops(dz, NZ) == reach] if reach < NZ // 2 else []
     for dz in relays:
         pl.semaphore_signal(r.far, inc=1, device_id=at_z(dz)[1], device_id_type=MESH)
 
-    for step in plane_steps:
-        yy, xx, _, device = at_plane(*step)
-        send(r.blocks.at[yy * NX + xx], r.slab.at[plane], "A", device)
-    r.slab[plane] = r.blocks[y * NX + x]
-
+    xc = x * NC + c
+    slot = z * NXC + xc
+
+    def phase_a(f):
+        for step in plane_steps:
+            _, xx, cc, device = at_plane(*step)
+            send(r.blocks.at[f, xx * NC + cc], r.slab.at[f, plane], f"A{f}", device)
+        r.slab[f, plane] = r.blocks[f, xc]
+
+    phase_a(1)
+
+    order = z_steps + [0]
+    loads[4].wait()
+    loads[5].wait()
+    for n, dz in enumerate(order):
+        zd = (z + dz) % NZ
+        yv = r.yt[zd // s.zl]
+        xv = r.xt[zd % s.zl]
+        high, low = split(jnp.concatenate([xv] * NXC, axis=0) * yv)
+        r.th[n] = high
+        r.tl[n] = low
+
+    loads[2].wait()
+    r.fields[0] = r.inp[...].astype(F32).reshape(rows, 128)
+    make_blocks(0)
     local = lax.dot_general(
-        r.inp[...].astype(F32).reshape(rows, 128).astype(BF16),
+        r.fields[0].astype(BF16),
         r.grad[...],
         (((0,), (0,)), ((), ())),
         preferred_element_type=F32,
@@ -185,41 +203,41 @@
     rk = 128 // NP
     for n in range(NP):
         r.skip_a[n] = local[n * rk : (n + 1) * rk]
-    loads[4].wait()
-    loads[5].wait()
-
-    order = z_steps + [0]
-
-    def forward_table(n, dz):
-        zd = (z + dz) % NZ
-        yv = r.yt[zd // s.zl]
-        xv = r.xt[zd % s.zl]
-        for y2 in range(half):
-            prod = jnp.concatenate(
-                [xv[y2 * 2 + e : y2 * 2 + e + 1] * yv for e in range(2)], axis=0
-            )
-            high, low = split(prod)
-            r.th[n, pl.ds(y2 * 2 * NXC, 2 * NXC), :] = high
-            r.tl[n, pl.ds(y2 * 2 * NXC, 2 * NXC), :] = low
-
-    for n, dz in enumerate(order):
-        forward_table(n, dz)
-
-    wait(r.slab, NP - 1, "A", r.recv)
-    slab = r.slab[...].reshape(s.cells, 128)
+
+    def sheet(dzs):
+        steps = [(dz, dx, dc) for dz in dzs for dx in range(NX) for dc in range(NC)]
+        return sorted(
+            (t for t in steps if sum(t)), key=lambda t: -(hops(t[0], NZ) + hops(t[1], NX))
+        )
+
+    def at_sheet(dz, dx, dc):
+        zz, xx, cc = (z + dz) % NZ, (x + dx) % NX, (c + dc) % NC
+        return xx * NC + cc, (y * s.zl + zz % s.zl, (xx * s.zh + zz // s.zl) * NC + cc)
+
+    def phase_b(f, chunks):
+        slab = r.slab[f].reshape(s.cells, 128)
+        chunk = NZ // chunks
+        nm = chunk * 2 * NXC
+        for g in range(0, NZ, chunk):
+            parts = jnp.dot(
+                r.th[g : g + chunk].reshape(nm, s.cells), slab, preferred_element_type=F32
+            ) + jnp.dot(r.tl[g : g + chunk].reshape(nm, s.cells), slab, preferred_element_type=F32)
+            r.parts[f, g : g + chunk] = parts.astype(BF16).reshape(chunk, NXC, 2, 128)
+            for step in sheet(order[g : g + chunk]):
+                k, device = at_sheet(*step)
+                send(r.parts.at[f, order.index(step[0]), k], r.sums.at[f, slot], f"B{f}", device)
+        r.sums[f, slot] = r.parts[f, NZ - 1, xc]
+
+    row_steps = [t for t in plane_steps if t[0] == 0]
     if relays:
         pl.semaphore_wait(r.far, len(relays))
-    chunk = NZ // s.chunks
-    nm = chunk * half * 2 * NXC
-    for g in range(0, NZ, chunk):
-        parts = jnp.dot(
-            r.th[g : g + chunk].reshape(nm, s.cells), slab, preferred_element_type=F32
-        ) + jnp.dot(r.tl[g : g + chunk].reshape(nm, s.cells), slab, preferred_element_type=F32)
-        r.parts[g : g + chunk] = parts.astype(BF16).reshape(chunk, half * 2 * NXC, 128)
-        for n in range(g, min(g + chunk, NZ - 1)):
-            send(r.parts.at[n], r.sums.at[z], "B", at_z(order[n])[1])
-    r.sums[z] = r.parts[NZ - 1]
-
+    for step in row_steps:
+        pl.semaphore_signal(r.row, inc=1, device_id=at_plane(*step)[3], device_id_type=MESH)
+    wait(r.slab.at[1], NP - 1, "A1", r.recv)
+    pl.semaphore_wait(r.row, len(row_steps))
+    phase_b(1, s.chunks)
+
+    phase_a(0)
     for step in plane_steps:
         yy, xx, cc, device = at_plane(*step)
         send(r.skip_a.at[(yy * NX + xx) * NC + cc], r.skip_b.at[plane], "SA", device)
@@ -230,7 +248,6 @@
     )
     loads[6].wait()
     loads[7].wait()
-
     yorder = sorted(range(NY), key=lambda d: -hops(d, NY))
 
     @pl.loop(0, NP)
@@ -246,55 +263,26 @@
             r.uh[n, pl.ds(j * 8, 16), :] = high
             r.ul[n, pl.ds(j * 8, 16), :] = low
 
-    wait(r.sums, NZ - 1, "B", r.recv)
-    modes = jnp.sum(r.sums[...].astype(F32), axis=0)
-    for y2 in range(half):
-        for e in range(2):
-            for k in range(NXC):
-                row = (y2 * 2 + e) * NXC + k
-                r.own_a[y2 * NXC + k, e : e + 1, :] = modes[row : row + 1]
-    chip = y * NX + x
-    mine = y // half == c
-    for y2 in range(half):
-        for k in range(NXC):
-            yy = half * c + y2
-            xx, cc = (x + k // NC) % NX, (c + k % NC) % NC
-            device = (yy * s.zl + zl, (xx * s.zh + zh) * NC + cc)
-
-            def go(yy=yy, xx=xx, cc=cc, device=device, y2=y2):
-                send(r.own_a.at[y2 * NXC + xx * NC + cc], r.own_b.at[chip], "C", device)
-
-            if k == 0:
-                pl.when(yy != y)(go)
-            else:
-                go()
-
     wait(r.skip_b, NP - 1, "SA", r.recv)
     r.skip_c[...] = jnp.sum(r.skip_b[...], axis=0)
     for dz in z_steps:
-        zz, device = at_z(dz)
+        device = at_z(dz)[1]
         send(r.skip_c, r.skip_d.at[z], "SB", device)
     r.skip_d[z] = r.skip_c[...]
 
-    @pl.when(mine)
-    def _():
-        r.own_b[chip] = r.own_a[(y % half) * NXC + x * NC + c]
-        wait(r.own_b, NY * NX - 1, "C", r.recv)
-        wait(r.own_a, half * NXC - 1, "C", r.send)
-
-    @pl.when(jnp.logical_not(mine))
-    def _():
-        wait(r.own_b, NY * NX, "C", r.recv)
-        wait(r.own_a, half * NXC, "C", r.send)
-
-    for f in range(2):
-        vals = [r.own_b[f * NK + k] for k in range(NK)]
+    def owned(f):
+        wait(r.sums.at[f], NZ * NXC - 1, f"B{f}", r.recv)
+        total = jnp.sum(r.sums[f].reshape(NZ, 2 * NXC, 128).astype(F32), axis=0)
+        r.own[...] = total
+        vals = [r.own[2 * k : 2 * k + 2] for k in range(NK)]
         for m in range(NK):
             total = vals[0] * s.fz[m][0]
             for k in range(1, NK):
                 total += vals[k] * s.fz[m][k]
             r.modes[f, 2 * m : 2 * m + 2, :] = total
+
     loads[8].wait()
+    owned(1)
     gm = r.modes[1]
     high, low = split(gm)
     lhs = jnp.concatenate([high, low], axis=0)
@@ -306,35 +294,16 @@
             )
             row = 2 * m + e
             back = d[row : row + 1] + d[nr + row : nr + row + 1]
-            r.back_a[m, e : e + 1, :] = back.astype(BF16).astype(F32)
-
-    xc = x * NC + c
-    for dy, dx, dc in plane_steps:
-        if dy:
-            continue
-        xx, cc = (x + dx) % NX, (c + dc) % NC
-        device = (gx, (xx * s.zh + zh) * NC + cc)
-        send(r.back_a.at[xx * NC + cc], r.back_b.at[xc], "D", device)
-    r.back_b[xc] = r.back_a[xc]
-
-    im = jnp.transpose(r.modes[0], (1, 0))
-
-    def outer(lo, hi):
-        for row in range(lo, hi):
-            r.gs[row % 2, 0, row // 2] = (im[:, row : row + 1] * gm[row : row + 1]).astype(BF16)
-
-    outer(0, nr // 2)
-
-    wait(r.back_b, NXC - 1, "D", r.recv)
-    block = jnp.concatenate([r.back_b[:, e, :] for e in range(2)], axis=0).astype(BF16)
-    r.gather_a[...] = block
-    r.gather_b[z] = block
-    for dz in z_steps:
-        zz, device = at_z(dz)
-        send(r.gather_a, r.gather_b.at[z], "E", device)
-    outer(nr // 2, nr)
-    out = pltpu.make_async_copy(r.gs, gs, r.local.at[9])
-    out.start()
+            r.back[row : row + 1, :] = back
+    r.back_a[...] = r.back[...].astype(BF16).reshape(NK, 2, 128)
+
+    for step in sheet(order):
+        k, device = at_sheet(*step)
+        send(r.back_a.at[k], r.gather.at[slot], "D", device)
+    r.gather[slot] = r.back_a[xc]
+
+    wait(r.slab.at[0], NP - 1, "A0", r.recv)
+    phase_b(0, 1)
 
     wait(r.skip_d, NZ - 1, "SB", r.recv)
     r.skip_e[...] = jnp.sum(r.skip_d[...], axis=0) * s.scale
@@ -343,8 +312,8 @@
         send(r.skip_e, r.skip_f.at[plane], "SC", device)
     r.skip_f[plane] = r.skip_e[...]
 
-    wait(r.gather_b, NZ - 1, "E", r.recv)
-    gathered = r.gather_b[...].reshape(NZ * 2 * NXC, 128)
+    wait(r.gather, NZ * NXC - 1, "D", r.recv)
+    gathered = r.gather[...].reshape(NZ * 2 * NXC, 128)
     nc = NXC * 32
     for g, dy in enumerate(yorder):
         part = slice(g * NXC, (g + 1) * NXC)
@@ -357,6 +326,11 @@
                 _, xx, cc, device = at_plane(*step)
                 send(r.cells_a.at[g * NXC + xx * NC + cc], r.cells_b.at[plane], "F", device)
     r.cells_b[plane] = r.cells_a[yorder.index(0) * NXC + xc]
+
+    owned(0)
+    im = jnp.transpose(r.modes[0], (1, 0))
+    for row in range(nr):
+        gs[row % 2, 0, row // 2] = (im[:, row : row + 1] * gm[row : row + 1]).astype(BF16)
 
     wait(r.skip_f, NP - 1, "SC", r.recv)
     gk[...] = r.skip_f[...]
@@ -377,17 +351,17 @@
     gi[...] = (r.fields[0] + r.skip[...]).astype(BF16).reshape(gi.shape)
 
     for ref, count, name in (
-        (r.slab, NP - 1, "A"),
+        (r.slab.at[1], NP - 1, "A1"),
+        (r.slab.at[0], NP - 1, "A0"),
         (r.skip_a, NP - 1, "SA"),
-        (r.sums, NZ - 1, "B"),
+        (r.sums.at[1], NZ * NXC - 1, "B1"),
+        (r.sums.at[0], NZ * NXC - 1, "B0"),
         (r.skip_d, NZ - 1, "SB"),
-        (r.back_b, NXC - 1, "D"),
-        (r.gather_b, NZ - 1, "E"),
+        (r.gather, NZ * NXC - 1, "D"),
         (r.skip_f, NP - 1, "SC"),
         (r.cells_b, NP - 1, "F"),
     ):
         wait(ref, count, name, r.send)
-    out.wait()
 
 
 def solution(mesh):
@@ -395,8 +369,8 @@
         nk = inputs.shape[2]
         gx, gy = mesh.shape["gx"], mesh.shape["gy"]
         zl, zh = gx // NY, gy // (NX * NC)
-        nz, np_, half, nxc = zl * zh, NY * NX * NC, NY // NC, NX * NC
-        names = ("A", "SA", "B", "SB", "C", "D", "E", "SC", "F")
+        nz, np_, nxc = zl * zh, NY * NX * NC, NX * NC
+        names = ("A0", "A1", "SA", "B0", "B1", "SB", "D", "SC", "F")
         table = cas(nk, nk)
         s = SimpleNamespace(
             gx=gx,
@@ -419,7 +393,6 @@
             cot=V(inputs.shape, BF16),
             skw=V((128, 128), BF16),
             w=V(spectral_w.shape, BF16),
-            gs=V(spectral_w.shape, BF16),
             xt=V(tables[0].shape[2:], F32),
             yt=V(tables[1].shape[1:], F32),
             at=V(tables[2].shape[2:], F32),
@@ -427,19 +400,17 @@
             fields=V((2, 32 * nk, 128), F32),
             grad=V((32 * nk, 128), BF16),
             skip=V((32 * nk, 128), F32),
-            blocks=V((2 * nk, 32, 128), BF16),
-            slab=V((np_, 32, 128), BF16),
-            th=V((nz, half * 2 * nxc, s.cells), BF16),
-            tl=V((nz, half * 2 * nxc, s.cells), BF16),
-            parts=V((nz, half * 2 * nxc, 128), BF16),
-            sums=V((nz, half * 2 * nxc, 128), BF16),
-            own_a=V((half * nxc, 2, 128), F32),
-            own_b=V((NY * NX, 2, 128), F32),
+            blocks=V((2, nk, 32, 128), BF16),
+            slab=V((2, np_, 32, 128), BF16),
+            th=V((nz, 2 * nxc, s.cells), BF16),
+            tl=V((nz, 2 * nxc, s.cells), BF16),
+            parts=V((2, nz, nxc, 2, 128), BF16),
+            sums=V((2, nz * nxc, 2, 128), BF16),
+            own=V((2 * nxc, 128), F32),
             modes=V((2, 2 * nk, 128), F32),
-            back_a=V((nk, 2, 128), F32),
-            back_b=V((nxc, 2, 128), F32),
-            gather_a=V((2 * nxc, 128), BF16),
-            gather_b=V((nz, 2 * nxc, 128), BF16),
+            back=V((2 * nk, 128), F32),
+            back_a=V((nk, 2, 128), BF16),
+            gather=V((nz * nxc, 2, 128), BF16),
             uh=V((np_, 32, nz * 2 * nxc), BF16),
             ul=V((np_, 32, nz * 2 * nxc), BF16),
             cells_a=V((np_, 32, 128), BF16),
@@ -452,8 +423,9 @@
             skip_f=V((np_, rk, 128), F32),
             send=pltpu.SemaphoreType.DMA((len(names),)),
             recv=pltpu.SemaphoreType.DMA((len(names),)),
-            local=pltpu.SemaphoreType.DMA((10,)),
+            local=pltpu.SemaphoreType.DMA((9,)),
             far=pltpu.SemaphoreType.REGULAR,
+            row=pltpu.SemaphoreType.REGULAR,
         )
 
         def body(*refs):
@@ -469,7 +441,7 @@
                 jax.ShapeDtypeStruct((np_, rk, 128), F32),
             ),
             in_specs=[pl.BlockSpec(memory_space=pltpu.HBM)] * 9,
-            out_specs=(vmem, any_space, vmem),
+            out_specs=(vmem, vmem, vmem),
             scratch_shapes=list(scratch.values()),
             compiler_params=pltpu.CompilerParams(
                 collective_id=0, has_side_effects=True, vmem_limit_bytes=16 << 20

time: 52.8 us -> 48.7 us (0.922)
  Pallas kernels: 52 us -> 47.9 us
    pallas_call x1, Pallas kernels: 51.2 us -> 47.1 us  [on_device(): pl.pallas_call(body, out_shape=(jax.ShapeDtypeStruct(inputs.shape, BF16),...]
where the time goes in v4:
time: 48.7 us; the launch traced here: 48.5 us
  Pallas kernels  47.9 us (98%)
  between operations  0.64 us (1%)
    pallas_call x1, Pallas kernels, on_device(): pl.pallas_call(body, out_shape=(jax.ShapeDtypeStruct(inputs.shape, BF16),...  47.1 us

profile of v4, /device:TPU:1, one launch (start us, length us, event | category | flops | bytes accessed | tf_op | source)
XLA Modules:
  0.0 48.5 jit_solution(16744489842200508923)
XLA Ops:
  0.6 47.1 %layer.1 = (bf16[8,4,8,128]{3,2,1,0:T(8,128)(2,1)S(1)}, bf16[2,1,8,128,128]{4,3,2,1,0:T(8,128)(2,1)S(1)}, f32[32,4,128]{2,1,0:T(4,128)S(1)}) custom-call(bf16[8,4,8,128]{3,2,1,0:T(8,128)(2,1)} %refs_0_.1, bf16[8,4,8,128]{3,2,1,0:T(8,128)(2,1)} %refs_1_.1, bf16[8,4,8,128]{3,2,1,0:T(8,128)(2,1)} %refs_2_.1, bf16[2,1,8,128,128]{4,3,2,1,0:T(8,128)(2,1)} %refs_3_.1, ...), custom_call_target="tpu_custom_call" | custom-call | tf_op jit(solution)/shard_map/layer/pallas_call | solution.py:436
  47.7 0.9 %store.1 = (bf16[8,4,8,128]{3,2,1,0:T(8,128)(2,1)}, bf16[2,1,8,128,128]{4,3,2,1,0:T(8,128)(2,1)}, f32[128,128]{1,0:T(8,128)}) custom-call(bf16[8,4,8,128]{3,2,1,0:T(8,128)(2,1)S(1)} %get-tuple-element.6.refs_0_, bf16[2,1,8,128,128]{4,3,2,1,0:T(8,128)(2,1)S(1)} %get-tuple-element.7.refs_1_, f32[128,128]{1,0:T(8,128)S(1)} %bitcast.1), custom_call_target="tpu_custom_call" | custom-call | tf_op jit(solution)/shard_map/store/pallas_call | solution.py:465

commit v5 on v4

--- a/solution.py
+++ b/solution.py
@@ -237,7 +237,6 @@
     pl.semaphore_wait(r.row, len(row_steps))
     phase_b(1, s.chunks)
 
-    phase_a(0)
     for step in plane_steps:
         yy, xx, cc, device = at_plane(*step)
         send(r.skip_a.at[(yy * NX + xx) * NC + cc], r.skip_b.at[plane], "SA", device)
@@ -264,6 +263,7 @@
             r.ul[n, pl.ds(j * 8, 16), :] = low
 
     wait(r.skip_b, NP - 1, "SA", r.recv)
+    phase_a(0)
     r.skip_c[...] = jnp.sum(r.skip_b[...], axis=0)
     for dz in z_steps:
         device = at_z(dz)[1]

time: 48.7 us -> 45.8 us (0.940)
  Pallas kernels: 47.9 us -> 45 us
    pallas_call x1, Pallas kernels: 47.1 us -> 44.2 us  [on_device(): pl.pallas_call(body, out_shape=(jax.ShapeDtypeStruct(inputs.shape, BF16),...]
where the time goes in v5:
time: 45.8 us; the launch traced here: 45.7 us
  Pallas kernels  45 us (98%)
  between operations  0.64 us (1%)
    pallas_call x1, Pallas kernels, on_device(): pl.pallas_call(body, out_shape=(jax.ShapeDtypeStruct(inputs.shape, BF16),...  44.2 us

profile of v5, /device:TPU:1, one launch (start us, length us, event | category | flops | bytes accessed | tf_op | source)
XLA Modules:
  0.0 45.7 jit_solution(15338471781022484397)
XLA Ops:
  0.6 44.2 %layer.1 = (bf16[8,4,8,128]{3,2,1,0:T(8,128)(2,1)S(1)}, bf16[2,1,8,128,128]{4,3,2,1,0:T(8,128)(2,1)S(1)}, f32[32,4,128]{2,1,0:T(4,128)S(1)}) custom-call(bf16[8,4,8,128]{3,2,1,0:T(8,128)(2,1)} %refs_0_.1, bf16[8,4,8,128]{3,2,1,0:T(8,128)(2,1)} %refs_1_.1, bf16[8,4,8,128]{3,2,1,0:T(8,128)(2,1)} %refs_2_.1, bf16[2,1,8,128,128]{4,3,2,1,0:T(8,128)(2,1)} %refs_3_.1, ...), custom_call_target="tpu_custom_call" | custom-call | tf_op jit(solution)/shard_map/layer/pallas_call | solution.py:436
  44.8 0.9 %store.1 = (bf16[8,4,8,128]{3,2,1,0:T(8,128)(2,1)}, bf16[2,1,8,128,128]{4,3,2,1,0:T(8,128)(2,1)}, f32[128,128]{1,0:T(8,128)}) custom-call(bf16[8,4,8,128]{3,2,1,0:T(8,128)(2,1)S(1)} %get-tuple-element.6.refs_0_, bf16[2,1,8,128,128]{4,3,2,1,0:T(8,128)(2,1)S(1)} %get-tuple-element.7.refs_1_, f32[128,128]{1,0:T(8,128)S(1)} %bitcast.1), custom_call_target="tpu_custom_call" | custom-call | tf_op jit(solution)/shard_map/store/pallas_call | solution.py:465

commit v6 on v5

--- a/solution.py
+++ b/solution.py
@@ -302,15 +302,15 @@
         send(r.back_a.at[k], r.gather.at[slot], "D", device)
     r.gather[slot] = r.back_a[xc]
 
-    wait(r.slab.at[0], NP - 1, "A0", r.recv)
-    phase_b(0, 1)
-
     wait(r.skip_d, NZ - 1, "SB", r.recv)
     r.skip_e[...] = jnp.sum(r.skip_d[...], axis=0) * s.scale
     for step in plane_steps:
         device = at_plane(*step)[3]
         send(r.skip_e, r.skip_f.at[plane], "SC", device)
     r.skip_f[plane] = r.skip_e[...]
+
+    wait(r.slab.at[0], NP - 1, "A0", r.recv)
+    phase_b(0, 1)
 
     wait(r.gather, NZ * NXC - 1, "D", r.recv)
     gathered = r.gather[...].reshape(NZ * 2 * NXC, 128)

time: 45.8 us -> 45.8 us (level)
  no operation moved by 1% of the time
where the time goes in v6:
time: 45.8 us; the launch traced here: 45.7 us
  Pallas kernels  45.1 us (98%)
  between operations  0.64 us (1%)
    pallas_call x1, Pallas kernels, on_device(): pl.pallas_call(body, out_shape=(jax.ShapeDtypeStruct(inputs.shape, BF16),...  44.2 us

profile of v6, /device:TPU:1, one launch (start us, length us, event | category | flops | bytes accessed | tf_op | source)
XLA Modules:
  0.0 45.7 jit_solution(10259797436348409247)
XLA Ops:
  0.6 44.2 %layer.1 = (bf16[8,4,8,128]{3,2,1,0:T(8,128)(2,1)S(1)}, bf16[2,1,8,128,128]{4,3,2,1,0:T(8,128)(2,1)S(1)}, f32[32,4,128]{2,1,0:T(4,128)S(1)}) custom-call(bf16[8,4,8,128]{3,2,1,0:T(8,128)(2,1)} %refs_0_.1, bf16[8,4,8,128]{3,2,1,0:T(8,128)(2,1)} %refs_1_.1, bf16[8,4,8,128]{3,2,1,0:T(8,128)(2,1)} %refs_2_.1, bf16[2,1,8,128,128]{4,3,2,1,0:T(8,128)(2,1)} %refs_3_.1, ...), custom_call_target="tpu_custom_call" | custom-call | tf_op jit(solution)/shard_map/layer/pallas_call | solution.py:436
  44.8 0.9 %store.1 = (bf16[8,4,8,128]{3,2,1,0:T(8,128)(2,1)}, bf16[2,1,8,128,128]{4,3,2,1,0:T(8,128)(2,1)}, f32[128,128]{1,0:T(8,128)}) custom-call(bf16[8,4,8,128]{3,2,1,0:T(8,128)(2,1)S(1)} %get-tuple-element.6.refs_0_, bf16[2,1,8,128,128]{4,3,2,1,0:T(8,128)(2,1)S(1)} %get-tuple-element.7.refs_1_, f32[128,128]{1,0:T(8,128)S(1)} %bitcast.1), custom_call_target="tpu_custom_call" | custom-call | tf_op jit(solution)/shard_map/store/pallas_call | solution.py:465
